TPU v7x, 32 devices: a whole 2x2x4 slice. The times are simulated.
32 devices in a mesh: head: 2 (over y), blk: 16 (over z, x, core).
Axes of the slice: x: 2, y: 2, z: 4, core: 2. Of those that a mesh axis runs over, the one named last changes fastest.
Arguments:
- tokens: bfloat16 [4096, 1024], P(('blk', 'head')), may hold values from -6 to 6
- segments: int32 [4096], replicated, may hold values from 0 to 23, never falling along the last dimension, each value on 1 to 2560 neighbouring positions
- cotangent: bfloat16 [4096, 1024], P(('blk', 'head')), may hold values from -6 to 6
- w_query: bfloat16 [1024, 1024], P(('head', 'blk')), may hold values from -0.1875 to 0.1875
- w_key: bfloat16 [1024, 1024], P(('head', 'blk')), may hold values from -0.1875 to 0.1875
- w_value: bfloat16 [1024, 1024], P(('head', 'blk')), may hold values from -0.1875 to 0.1875
- b_query: bfloat16 [1024], P(('head', 'blk')), may hold values from -3 to 3
- b_value: bfloat16 [1024], P(('head', 'blk')), may hold values from -3 to 3
- w_output: bfloat16 [1024, 1024], P(('head', 'blk')), may hold values from -1.5 to 1.5
- b_output: bfloat16 [1024], P(('head', 'blk')), may hold values from -3 to 3
- gain_attn: bfloat16 [1024], P(('head', 'blk')), may hold values from 0.5 to 1.5
- shift_attn: bfloat16 [1024], P(('head', 'blk')), may hold values from -2 to 2
- w_inner: bfloat16 [1024, 4096], P(('head', 'blk')), may hold values from -0.1875 to 0.1875
- b_inner: bfloat16 [4096], P(('head', 'blk')), may hold values from -3 to 3
- w_outer: bfloat16 [4096, 1024], P(('head', 'blk')), may hold values from -0.09375 to 0.09375
- b_outer: bfloat16 [1024], P(('head', 'blk')), may hold values from -3 to 3
- gain_ffn: bfloat16 [1024], P(('head', 'blk')), may hold values from 0.5 to 1.5
- shift_ffn: bfloat16 [1024], P(('head', 'blk')), may hold values from -2 to 2
Outputs:
- out_rows: bfloat16 [4096, 1024], P(('blk', 'head'))
- grad_tokens: float32 [4096, 1024], P(('blk', 'head'))
- grad_wq: float32 [1024, 1024], P(('head', 'blk'))
- grad_wk: float32 [1024, 1024], P(('head', 'blk'))
- grad_wv: float32 [1024, 1024], P(('head', 'blk'))
- grad_bq: float32 [1024], P(('head', 'blk'))
- grad_bv: float32 [1024], P(('head', 'blk'))
- grad_wo: float32 [1024, 1024], P(('head', 'blk'))
- grad_bo: float32 [1024], P(('head', 'blk'))
- grad_g1: float32 [1024], P(('head', 'blk'))
- grad_n1: float32 [1024], P(('head', 'blk'))
- grad_w1: float32 [1024, 4096], P(('head', 'blk'))
- grad_b1: float32 [4096], P(('head', 'blk'))
- grad_w2: float32 [4096, 1024], P(('head', 'blk'))
- grad_b2: float32 [1024], P(('head', 'blk'))
- grad_g2: float32 [1024], P(('head', 'blk'))
- grad_n2: float32 [1024], P(('head', 'blk'))
Inputs may be any that keep to these rules, and one draw needn't show every extreme that they name: `segments`: segment numbers never fall along the stream; each document holds 1 to 2560 tokens, and one holds exactly 2560.
All inputs are finite; a program needn't handle non-finite values.
Results may differ from a plain program's by a relative error of at most 0.019.
Values may be sent and summed in bfloat16 or wider, within the bound.
No kernel may reach another device: no remote copies, remote signals or barrier semaphores. Data moves between devices by JAX's collectives and lax.ppermute only.
A program may use at most 192 MiB of HBM per device.

v0:
```python
import math
import jax
import jax.numpy as jnp
from jax import lax
from jax.sharding import PartitionSpec as P

H = 16
HD = 64
EPS = 1e-05
NEG = -1e30


def passed_along(value, axis, steps):
    count = lax.axis_size(axis)
    pairs = [(source, (source + steps) % count) for source in range(count)]
    return lax.ppermute(value, axis, pairs)


def layer_norm(hidden, gain_row, shift_row):
    centre = hidden - jnp.mean(hidden, axis=-1, keepdims=True)
    spread = jnp.mean(centre * centre, axis=-1, keepdims=True)
    return centre * lax.rsqrt(spread + EPS) * gain_row + shift_row


def exact_gelu(values):
    return jax.nn.gelu(values, approximate=False)


def row_sum(matrix):
    return jnp.sum(matrix.astype(jnp.float32), axis=0)


def left_product(former, latter):
    return lax.dot_general(
        former, latter, (((0,), (0,)), ((), ())), preferred_element_type=jnp.float32
    )


def right_product(former, latter):
    return lax.dot_general(
        former, latter, (((1,), (1,)), ((), ())), preferred_element_type=jnp.float32
    )


def intersections(query_segs, key_segs):
    return jnp.logical_and(key_segs[0] <= query_segs[-1], query_segs[0] <= key_segs[-1])


def fold_block(running, block_item, query_heads, query_segs, score_scale):
    key_block, value_block, key_segs = block_item
    running_max, weight_sum, mixed = running
    scores = (
        jnp.einsum("qgd,kgd->gqk", query_heads, key_block, preferred_element_type=jnp.float32)
        * score_scale
    )
    same = query_segs[:, None] == key_segs[None, :]
    scores = jnp.where(same[None], scores, NEG)
    new_max = jnp.maximum(running_max, jnp.max(scores, axis=-1))
    factor = jnp.exp(running_max - new_max)
    expo = jnp.exp(scores - new_max[:, :, None])
    weight_sum = weight_sum * factor + jnp.sum(expo, axis=-1)
    mixed = mixed * factor[:, :, None] + jnp.einsum(
        "gqk,kgd->gqd", expo.astype(jnp.bfloat16), value_block, preferred_element_type=jnp.float32
    )
    return (new_max, weight_sum, mixed)


def pair_terms(
    query_blk, grad_blk, log_blk, delta_blk, query_segs, key_blk, value_blk, key_segs, score_scale
):
    scores = (
        jnp.einsum("qgd,kgd->gqk", query_blk, key_blk, preferred_element_type=jnp.float32)
        * score_scale
    )
    same = query_segs[:, None] == key_segs[None, :]
    scores = jnp.where(same[None], scores, NEG)
    prob = jnp.exp(scores - log_blk[:, :, None])
    grad_prob = jnp.einsum("qgd,kgd->gqk", grad_blk, value_blk, preferred_element_type=jnp.float32)
    grad_score = (prob * (grad_prob - delta_blk[:, :, None])).astype(jnp.bfloat16)
    value_term = jnp.einsum(
        "gqk,qgd->kgd", prob.astype(jnp.bfloat16), grad_blk, preferred_element_type=jnp.float32
    )
    key_term = (
        jnp.einsum("gqk,qgd->kgd", grad_score, query_blk, preferred_element_type=jnp.float32)
        * score_scale
    )
    query_term = (
        jnp.einsum("gqk,kgd->qgd", grad_score, key_blk, preferred_element_type=jnp.float32)
        * score_scale
    )
    return (key_term, value_term, query_term)


def body(
    tokens,
    segments,
    cotangent,
    w_query,
    w_key,
    w_value,
    b_query,
    b_value,
    w_output,
    b_output,
    gain_attn,
    shift_attn,
    w_inner,
    b_inner,
    w_outer,
    b_outer,
    gain_ffn,
    shift_ffn,
):
    gathered = (
        lax.all_gather(w_query, ("head", "blk"), axis=0, tiled=True),
        lax.all_gather(w_key, ("head", "blk"), axis=0, tiled=True),
        lax.all_gather(w_value, ("head", "blk"), axis=0, tiled=True),
        lax.all_gather(b_query, ("head", "blk"), axis=0, tiled=True),
        lax.all_gather(b_value, ("head", "blk"), axis=0, tiled=True),
        lax.all_gather(w_output, ("head", "blk"), axis=0, tiled=True),
        lax.all_gather(b_output, ("head", "blk"), axis=0, tiled=True),
        lax.all_gather(gain_attn, ("head", "blk"), axis=0, tiled=True),
        lax.all_gather(shift_attn, ("head", "blk"), axis=0, tiled=True),
        lax.all_gather(w_inner, ("head", "blk"), axis=0, tiled=True),
        lax.all_gather(b_inner, ("head", "blk"), axis=0, tiled=True),
        lax.all_gather(w_outer, ("head", "blk"), axis=0, tiled=True),
        lax.all_gather(b_outer, ("head", "blk"), axis=0, tiled=True),
        lax.all_gather(gain_ffn, ("head", "blk"), axis=0, tiled=True),
        lax.all_gather(shift_ffn, ("head", "blk"), axis=0, tiled=True),
    )
    (
        full_wq,
        full_wk,
        full_wv,
        full_bq,
        full_bv,
        full_wo,
        full_bo,
        full_g1,
        full_n1,
        full_w1,
        full_b1,
        full_w2,
        full_b2,
        full_g2,
        full_n2,
    ) = gathered
    head_count = lax.axis_size("head")
    cycle_size = lax.axis_size("blk")
    head_group = H // head_count
    head_width = head_group * HD
    score_scale = HD ** (-0.5)
    inputs = tokens.astype(jnp.float32)
    query_tok = (
        jnp.dot(tokens, full_wq, preferred_element_type=jnp.float32) + full_bq.astype(jnp.float32)
    ).astype(jnp.bfloat16)
    key_tok = jnp.dot(tokens, full_wk, preferred_element_type=jnp.float32).astype(jnp.bfloat16)
    value_tok = (
        jnp.dot(tokens, full_wv, preferred_element_type=jnp.float32) + full_bv.astype(jnp.float32)
    ).astype(jnp.bfloat16)
    query_cols, key_cols, value_cols = (
        lax.all_to_all(query_tok, "head", split_axis=1, concat_axis=0, tiled=True),
        lax.all_to_all(key_tok, "head", split_axis=1, concat_axis=0, tiled=True),
        lax.all_to_all(value_tok, "head", split_axis=1, concat_axis=0, tiled=True),
    )
    row_count = query_cols.shape[0]
    cycle_index = lax.axis_index("blk")
    query_segs = lax.dynamic_slice_in_dim(segments, cycle_index * row_count, row_count)
    query_heads = query_cols.reshape(row_count, head_group, HD)
    initial = (
        jnp.full((head_group, row_count), NEG, jnp.float32),
        jnp.zeros((head_group, row_count), jnp.float32),
        jnp.zeros((head_group, row_count, HD), jnp.float32),
    )
    running = initial
    key_piece = lax.all_gather(key_cols, "blk", axis=0, tiled=True)
    value_piece = lax.all_gather(value_cols, "blk", axis=0, tiled=True)
    piece_rows = key_piece.shape[0]
    block_rows = math.gcd(piece_rows, 1024)
    block_count = piece_rows // block_rows
    key_segs = segments
    stacked = (
        key_piece.reshape(block_count, block_rows, head_group, HD),
        value_piece.reshape(block_count, block_rows, head_group, HD),
        key_segs.reshape(block_count, block_rows),
    )

    def visit(current, block_item):

        def update(inner_state):
            return fold_block(inner_state, block_item, query_heads, query_segs, score_scale)

        def visit_unchanged(inner_state):
            return inner_state

        current = lax.cond(
            intersections(query_segs, block_item[2]), update, visit_unchanged, current
        )
        return (current, None)

    running, _ = lax.scan(visit, running, stacked)
    running_max, weight_sum, mixed = running
    log_sum = running_max + jnp.log(weight_sum)
    context = jnp.transpose(mixed / weight_sum[:, :, None], (1, 0, 2))
    context_cols = context.astype(jnp.bfloat16).reshape(row_count, head_width)
    context_tok = lax.all_to_all(context_cols, "head", split_axis=0, concat_axis=1, tiled=True)
    attn_out = jnp.dot(context_tok, full_wo, preferred_element_type=jnp.float32) + full_bo.astype(
        jnp.float32
    )
    resid_one = inputs + attn_out
    norm_one = layer_norm(resid_one, full_g1.astype(jnp.float32), full_n1.astype(jnp.float32))
    inner_in = norm_one.astype(jnp.bfloat16)
    pre_act = jnp.dot(inner_in, full_w1, preferred_element_type=jnp.float32) + full_b1.astype(
        jnp.float32
    )
    activation = exact_gelu(pre_act).astype(jnp.bfloat16)
    outer_out = jnp.dot(activation, full_w2, preferred_element_type=jnp.float32) + full_b2.astype(
        jnp.float32
    )
    resid_two = norm_one + outer_out
    out_rows = layer_norm(
        resid_two, full_g2.astype(jnp.float32), full_n2.astype(jnp.float32)
    ).astype(jnp.bfloat16)
    back_wq, back_wk, back_wv, back_wo, back_w1, back_w2, back_g1, back_g2 = (
        lax.all_gather(w_query, ("head", "blk"), axis=0, tiled=True),
        lax.all_gather(w_key, ("head", "blk"), axis=0, tiled=True),
        lax.all_gather(w_value, ("head", "blk"), axis=0, tiled=True),
        lax.all_gather(w_output, ("head", "blk"), axis=0, tiled=True),
        lax.all_gather(w_inner, ("head", "blk"), axis=0, tiled=True),
        lax.all_gather(w_outer, ("head", "blk"), axis=0, tiled=True),
        lax.all_gather(gain_attn, ("head", "blk"), axis=0, tiled=True),
        lax.all_gather(gain_ffn, ("head", "blk"), axis=0, tiled=True),
    )
    _, back_two = jax.vjp(
        layer_norm, resid_two, back_g2.astype(jnp.float32), full_n2.astype(jnp.float32)
    )
    grad_resid_two, grad_g2, grad_n2 = back_two(cotangent.astype(jnp.float32))
    grad_outer = grad_resid_two.astype(jnp.bfloat16)
    grad_b2 = row_sum(grad_outer)
    grad_w2 = left_product(activation, grad_outer)
    grad_act = right_product(grad_outer, back_w2)
    _, gelu_back = jax.vjp(exact_gelu, pre_act)
    grad_pre = gelu_back(grad_act)[0].astype(jnp.bfloat16)
    grad_b1 = row_sum(grad_pre)
    grad_w1 = left_product(inner_in, grad_pre)
    grad_norm_one = grad_resid_two + right_product(grad_pre, back_w1)
    _, back_one = jax.vjp(
        layer_norm, resid_one, back_g1.astype(jnp.float32), full_n1.astype(jnp.float32)
    )
    grad_resid_one, grad_g1, grad_n1 = back_one(grad_norm_one)
    grad_attn = grad_resid_one.astype(jnp.bfloat16)
    grad_bo = row_sum(grad_attn)
    grad_wo = left_product(context_tok, grad_attn)
    grad_context = right_product(grad_attn, back_wo).astype(jnp.bfloat16)
    grad_cols = lax.all_to_all(grad_context, "head", split_axis=1, concat_axis=0, tiled=True)
    grad_heads = grad_cols.reshape(row_count, head_group, HD)
    delta_rows = jnp.transpose(jnp.sum(grad_heads.astype(jnp.float32) * context, axis=-1))
    key_heads = key_cols.reshape(row_count, head_group, HD)
    value_heads = value_cols.reshape(row_count, head_group, HD)
    zero_grad = jnp.zeros((row_count, head_group, HD), jnp.float32)

    def cycle_turn(turn_index, cycle_state):
        key_now, value_now, key_grad, value_grad, query_grad = cycle_state
        source = jnp.mod(cycle_index - turn_index, cycle_size)
        key_segs = lax.dynamic_slice_in_dim(segments, source * row_count, row_count)

        def pair_grads(grad_parts):
            part_key, part_value, part_query = grad_parts
            key_term, value_term, query_term = pair_terms(
                query_heads,
                grad_heads,
                log_sum,
                delta_rows,
                query_segs,
                key_now,
                value_now,
                key_segs,
                score_scale,
            )
            return (part_key + key_term, part_value + value_term, part_query + query_term)

        def cycle_unchanged(grad_parts):
            return grad_parts

        key_grad, value_grad, query_grad = lax.cond(
            intersections(query_segs, key_segs),
            pair_grads,
            cycle_unchanged,
            (key_grad, value_grad, query_grad),
        )
        key_now, value_now = passed_along((key_now, value_now), "blk", 1)
        key_grad, value_grad = (
            passed_along(key_grad.astype(jnp.bfloat16), "blk", 1).astype(key_grad.dtype),
            passed_along(value_grad.astype(jnp.bfloat16), "blk", 1).astype(value_grad.dtype),
        )
        return (key_now, value_now, key_grad, value_grad, query_grad)

    final_state = lax.fori_loop(
        0, cycle_size, cycle_turn, (key_heads, value_heads, zero_grad, zero_grad, zero_grad)
    )
    grad_key_heads = final_state[2]
    grad_value_heads = final_state[3]
    grad_query_heads = final_state[4]
    grad_query_tok, grad_key_tok, grad_value_tok = (
        lax.all_to_all(
            grad_query_heads.astype(jnp.bfloat16).reshape(row_count, head_width),
            "head",
            split_axis=0,
            concat_axis=1,
            tiled=True,
        ),
        lax.all_to_all(
            grad_key_heads.astype(jnp.bfloat16).reshape(row_count, head_width),
            "head",
            split_axis=0,
            concat_axis=1,
            tiled=True,
        ),
        lax.all_to_all(
            grad_value_heads.astype(jnp.bfloat16).reshape(row_count, head_width),
            "head",
            split_axis=0,
            concat_axis=1,
            tiled=True,
        ),
    )
    grad_bq = row_sum(grad_query_tok)
    grad_bv = row_sum(grad_value_tok)
    grad_wq = left_product(tokens, grad_query_tok)
    grad_wk = left_product(tokens, grad_key_tok)
    grad_wv = left_product(tokens, grad_value_tok)
    grad_tokens = (
        grad_resid_one
        + right_product(grad_query_tok, back_wq)
        + right_product(grad_key_tok, back_wk)
        + right_product(grad_value_tok, back_wv)
    )
    shards = (
        lax.psum_scatter(grad_wq, ("head", "blk"), scatter_dimension=0, tiled=True),
        lax.psum_scatter(grad_wk, ("head", "blk"), scatter_dimension=0, tiled=True),
        lax.psum_scatter(grad_wv, ("head", "blk"), scatter_dimension=0, tiled=True),
        lax.psum_scatter(grad_bq, ("head", "blk"), scatter_dimension=0, tiled=True),
        lax.psum_scatter(grad_bv, ("head", "blk"), scatter_dimension=0, tiled=True),
        lax.psum_scatter(grad_wo, ("head", "blk"), scatter_dimension=0, tiled=True),
        lax.psum_scatter(grad_bo, ("head", "blk"), scatter_dimension=0, tiled=True),
        lax.psum_scatter(grad_g1, ("head", "blk"), scatter_dimension=0, tiled=True),
        lax.psum_scatter(grad_n1, ("head", "blk"), scatter_dimension=0, tiled=True),
        lax.psum_scatter(grad_w1, ("head", "blk"), scatter_dimension=0, tiled=True),
        lax.psum_scatter(grad_b1, ("head", "blk"), scatter_dimension=0, tiled=True),
        lax.psum_scatter(grad_w2, ("head", "blk"), scatter_dimension=0, tiled=True),
        lax.psum_scatter(grad_b2, ("head", "blk"), scatter_dimension=0, tiled=True),
        lax.psum_scatter(grad_g2, ("head", "blk"), scatter_dimension=0, tiled=True),
        lax.psum_scatter(grad_n2, ("head", "blk"), scatter_dimension=0, tiled=True),
    )
    return (out_rows, grad_tokens) + tuple(shards)


def solution(mesh):
    placed = (
        P(("blk", "head"), None),
        P(),
        P(("blk", "head"), None),
        P(("head", "blk"), None),
        P(("head", "blk"), None),
        P(("head", "blk"), None),
        P(("head", "blk")),
        P(("head", "blk")),
        P(("head", "blk"), None),
        P(("head", "blk")),
        P(("head", "blk")),
        P(("head", "blk")),
        P(("head", "blk"), None),
        P(("head", "blk")),
        P(("head", "blk"), None),
        P(("head", "blk")),
        P(("head", "blk")),
        P(("head", "blk")),
    )
    return jax.shard_map(
        body,
        mesh=mesh,
        in_specs=placed,
        out_specs=(
            P(("blk", "head"), None),
            P(("blk", "head"), None),
            P(("head", "blk"), None),
            P(("head", "blk"), None),
            P(("head", "blk"), None),
            P(("head", "blk")),
            P(("head", "blk")),
            P(("head", "blk"), None),
            P(("head", "blk")),
            P(("head", "blk")),
            P(("head", "blk")),
            P(("head", "blk"), None),
            P(("head", "blk")),
            P(("head", "blk"), None),
            P(("head", "blk")),
            P(("head", "blk")),
            P(("head", "blk")),
        ),
        check_vma=False,
    )
```

profile of v0, /device:TPU:4, one launch (start us, length us, event | category | flops | bytes accessed | tf_op | source)
XLA Modules:
  0.0 1730.0 jit_solution(9327280273881781329)
XLA Ops:
  9.5 59.1 %all-gather.10.cloned.1.call-done = bf16[1024,1024]{1,0:T(8,128)(2,1)} async-done(((bf16[32,1024]{1,0:T(8,128)(2,1)}), bf16[1024,1024]{1,0:T(8,128)(2,1)}) %all-gather.10.cloned.1.call-update) | async-done | bytes 2097168 | tf_op jit(solution)/shard_map/all_gather | solution.py:116
  80.6 40.7 %all-reduce.18 = (bf16[1024]{0:T(1024)(128)(2,1)S(1)}, bf16[1024]{0:T(1024)(128)(2,1)S(1)}, bf16[1024]{0:T(1024)(128)(2,1)S(1)}, bf16[1024]{0:T(1024)(128)(2,1)S...) all-reduce(bf16[1024]{0:T(1024)(128)(2,1)S(1)} %dynamic-update-slic, ...), channel_id=1, replica_groups=mesh['head'=2,'blk'=16] {'head','blk'}, use_global_device_ids=true, to_apply=%add | all-reduce | flops 8192 | bytes 32768
  139.2 46.2 %all-gather.14.cloned.1.call-done = bf16[1024,1024]{1,0:T(8,128)(2,1)} async-done(((bf16[32,1024]{1,0:T(8,128)(2,1)}), bf16[1024,1024]{1,0:T(8,128)(2,1)}) %all-gather.14.cloned.1.call-update) | async-done | bytes 2097168 | tf_op jit(solution)/shard_map/all_gather | solution.py:115
  192.1 39.4 %all-gather = bf16[32,1,128]{2,1,0:T(2,128)(2,1)S(1)} all-gather(bf16[1,1,128]{2,1,0:T(2,128)(2,1)S(1)} %bitcast.197), channel_id=1, replica_groups=mesh['head'=2,'blk'=16] {'head','blk'}, dimensions={0}, use_global_device_ids=true | all-gather | bytes 8448 | tf_op jit(solution)/shard_map/all_gather | solution.py:125
  237.0 11.3 reshape.263
  248.3 9.9 copy.106
  258.2 30.1 %all-gather.18.cloned.1.call-done = bf16[4096,512]{1,0:T(8,128)(2,1)} async-done(((bf16[256,512]{1,0:T(8,128)(2,1)}), bf16[4096,512]{1,0:T(8,128)(2,1)}) %all-gather.18.cloned.1.call-update) | async-done | bytes 4194320 | tf_op jit(solution)/shard_map/all_gather | solution.py:177
  288.3 11.2 reshape.264
  299.5 9.8 copy.107
  309.3 23.4 %while.38 = (s32[]{:T(128)}, f32[8,256]{1,0:T(8,128)S(1)}, f32[8,256]{1,0:T(8,128)S(1)}, f32[8,256,64]{1,2,0:T(8,128)S(1)}, s32[4,1024]{1,0:T(4,128)S(1)}, /*ind...) while((s32[]{:T(128)}, f32[8,256]{1,0:T(8,128)S(1)}, ...), condition=%wide.region_5.6_spmd, body=%wide.region_0.5_spmd.sunk | while | flops 560467968 | bytes 29768016 | solution.py:201
  348.4 76.9 %all-gather.22.cloned.1.call-done = bf16[1024,4096]{1,0:T(8,128)(2,1)} async-done(((bf16[32,4096]{1,0:T(8,128)(2,1)}), bf16[1024,4096]{1,0:T(8,128)(2,1)}) %all-gather.22.cloned.1.call-update) | async-done | bytes 8388624 | tf_op jit(solution)/shard_map/all_gather | solution.py:124
  425.3 9.7 multiply_convert_fusion.1
  435.0 69.3 %all-gather.24.cloned.1.call-done = bf16[4096,1024]{1,0:T(8,128)(2,1)} async-done(((bf16[128,1024]{1,0:T(8,128)(2,1)}), bf16[4096,1024]{1,0:T(8,128)(2,1)}) %all-gather.24.cloned.1.call-update) | async-done | bytes 8388624 | tf_op jit(solution)/shard_map/all_gather | solution.py:126
  531.7 384.5 %while.39 = (s32[]{:T(128)}, bf16[256,8,64]{0,2,1:T(8,128)(2,1)}, bf16[256,8,64]{0,2,1:T(8,128)(2,1)S(1)}, f32[256,8,64]{0,2,1:T(8,128)S(1)}, f32[256,8,64]{0,2,...) while((s32[]{:T(128)}, bf16[256,8,64]{0,2,1:T(8,128)(2,1)}, ...), condition=%wide.region_18.19_spmd.clone, body=%wide.region_15.18_spmd.clone.sunk | while | flops 340721696 | bytes 25055948 | solution.py:298
  639.6 8.9 collective-permute-done.2
  664.7 8.9 collective-permute-done.2
  689.7 8.2 collective-permute-done.2
  712.7 8.2 collective-permute-done.2
  985.5 40.6 %all-reduce.17 = (f32[1024]{0:T(1024)S(1)}, f32[1024]{0:T(1024)S(1)}, f32[1024]{0:T(1024)S(1)}, f32[1024]{0:T(1024)S(1)}, f32[1024]{0:T(1024)S(1)}, /*index=5*/f...) all-reduce(f32[1024]{0:T(1024)S(1)} %bitcast.194, ...), channel_id=5, replica_groups=mesh['head'=2,'blk'=16] {'head','blk'}, use_global_device_ids=true, to_apply=%region_23.24.clone | all-reduce | flops 12288 | bytes 98304
  1035.5 34.0 %reduce-scatter.19.cloned.1.call-done = f32[32,1024]{1,0:T(8,128)} async-done(((f32[1024,1024]{1,0:T(8,128)}), f32[32,1024]{1,0:T(8,128)}) %reduce-scatter.19.cloned.1.call-update) | async-done | bytes 131088
  1069.6 140.6 %reduce-scatter.21.cloned.1.call-done = f32[32,1024]{1,0:T(8,128)} async-done(((f32[1024,1024]{1,0:T(8,128)}), f32[32,1024]{1,0:T(8,128)}) %reduce-scatter.21.cloned.1.call-update) | async-done | bytes 131088
  1210.2 140.4 %reduce-scatter.23.cloned.1.call-done = f32[32,1024]{1,0:T(8,128)} async-done(((f32[1024,1024]{1,0:T(8,128)}), f32[32,1024]{1,0:T(8,128)}) %reduce-scatter.23.cloned.1.call-update) | async-done | bytes 131088
  1350.6 185.6 %reduce-scatter.15.cloned.1.call-done = f32[32,4096]{1,0:T(8,128)} async-done(((f32[1024,4096]{1,0:T(8,128)}), f32[32,4096]{1,0:T(8,128)}) %reduce-scatter.15.cloned.1.call-update) | async-done | bytes 524304 | tf_op jit(solution)/shard_map/reduce_scatter | solution.py:348
  1536.3 186.9 %reduce-scatter.17.cloned.1.call-done = f32[128,1024]{1,0:T(8,128)} async-done(((f32[4096,1024]{1,0:T(8,128)}), f32[128,1024]{1,0:T(8,128)}) %reduce-scatter.17.cloned.1.call-update) | async-done | bytes 524304 | tf_op jit(solution)/shard_map/reduce_scatter | solution.py:350
  (565 shorter events, 498.9 us)
Async XLA Ops:
  7.3 61.4 %all-gather.10.cloned.1.call-start = ((), (), s32[]{:S(2)}) async-start(), calls=%async_computation.14 | async-start | bytes 2162688 | tf_op jit(solution)/shard_map/all_gather | solution.py:116
  8.0 119.1 %all-gather.16.cloned.1.call-start = ((), (), s32[]{:S(2)}) async-start(), calls=%async_computation.17 | async-start | bytes 2162688 | tf_op jit(solution)/shard_map/all_gather | solution.py:117
  8.8 176.6 %all-gather.14.cloned.1.call-start = ((), (), s32[]{:S(2)}) async-start(), calls=%async_computation.16 | async-start | bytes 2162688 | tf_op jit(solution)/shard_map/all_gather | solution.py:115
  9.5 227.5 %all-gather.12.cloned.1.call-start = ((), (), s32[]{:S(2)}) async-start(), calls=%async_computation.15 | async-start | bytes 4456448 | tf_op jit(solution)/shard_map/all_gather | solution.py:176
  78.6 209.7 %all-gather.18.cloned.1.call-start = ((), (), s32[]{:S(2)}) async-start(), calls=%async_computation.18 | async-start | bytes 4456448 | tf_op jit(solution)/shard_map/all_gather | solution.py:177
  137.0 208.9 %all-gather.20.cloned.1.call-start = ((), (), s32[]{:S(2)}) async-start(), calls=%async_computation.19 | async-start | bytes 2162688 | tf_op jit(solution)/shard_map/all_gather | solution.py:120
  137.6 287.7 %all-gather.22.cloned.1.call-start = ((), (), s32[]{:S(2)}) async-start(), calls=%async_computation.20 | async-start | bytes 8650752 | tf_op jit(solution)/shard_map/all_gather | solution.py:124
  138.4 365.8 %all-gather.24.cloned.1.call-start = ((), (), s32[]{:S(2)}) async-start(), calls=%async_computation.21 | async-start | bytes 8650752 | tf_op jit(solution)/shard_map/all_gather | solution.py:126
  188.1 43.5 %all-to-all-start.1 = ((bf16[128,2,512]{2,0,1:T(8,128)(2,1)}), bf16[128,2,512]{2,0,1:T(8,128)(2,1)S(1)}, u32[]{:S(2)}, u32[]{:S(2)}) async-start(bf16[128,2,512]{2,0,1:T(8,128)(2,1)} %bitcast.154), calls=%async_computation.1 | async-start | bytes 524288 | tf_op jit(solution)/shard_map/all_to_all | solution.py:162
  527.1 508.4 %reduce-scatter.13.cloned.1.call-start = ((), (), s32[]{:S(2)}) async-start(), calls=%async_computation.22 | async-start | bytes 4325376 | tf_op jit(solution)/shard_map/reduce_scatter | solution.py:344
  530.1 539.5 %reduce-scatter.19.cloned.1.call-start = ((), (), s32[]{:S(2)}) async-start(), calls=%async_computation.25 | async-start | bytes 4325376
  589.9 18.0 %collective-permute-start.1 = (bf16[256,8,64]{0,2,1:T(8,128)(2,1)S(1)}, bf16[256,8,64]{0,2,1:T(8,128)(2,1)S(1)}, u32[]{:S(2)}, u32[]{:S(2)}) collective-permute-start(bf16[256,8,64]{0,2,1:T(8,128)(2,1)S(1)} %copy.190), channel_id=1, source_target_pairs={{0,1},{1,2},{2,3},{3,4},{4,5},{5,6},{6,7},{7,8},{8,9},{9,10},{10,1... | collective-permute-start | bytes 786440 | tf_op jit(solution)/shard_map/while/body/eval_jaxpr/ppermute | solution.py:16
  614.2 19.1 %collective-permute-start.1 = (bf16[256,8,64]{0,2,1:T(8,128)(2,1)S(1)}, bf16[256,8,64]{0,2,1:T(8,128)(2,1)S(1)}, u32[]{:S(2)}, u32[]{:S(2)}) collective-permute-start(bf16[256,8,64]{0,2,1:T(8,128)(2,1)S(1)} %copy.190), channel_id=1, source_target_pairs={{0,1},{1,2},{2,3},{3,4},{4,5},{5,6},{6,7},{7,8},{8,9},{9,10},{10,1... | collective-permute-start | bytes 786440 | tf_op jit(solution)/shard_map/while/body/eval_jaxpr/ppermute | solution.py:16
  639.6 18.8 %collective-permute-start.1 = (bf16[256,8,64]{0,2,1:T(8,128)(2,1)S(1)}, bf16[256,8,64]{0,2,1:T(8,128)(2,1)S(1)}, u32[]{:S(2)}, u32[]{:S(2)}) collective-permute-start(bf16[256,8,64]{0,2,1:T(8,128)(2,1)S(1)} %copy.190), channel_id=1, source_target_pairs={{0,1},{1,2},{2,3},{3,4},{4,5},{5,6},{6,7},{7,8},{8,9},{9,10},{10,1... | collective-permute-start | bytes 786440 | tf_op jit(solution)/shard_map/while/body/eval_jaxpr/ppermute | solution.py:16
  664.6 18.8 %collective-permute-start.1 = (bf16[256,8,64]{0,2,1:T(8,128)(2,1)S(1)}, bf16[256,8,64]{0,2,1:T(8,128)(2,1)S(1)}, u32[]{:S(2)}, u32[]{:S(2)}) collective-permute-start(bf16[256,8,64]{0,2,1:T(8,128)(2,1)S(1)} %copy.190), channel_id=1, source_target_pairs={{0,1},{1,2},{2,3},{3,4},{4,5},{5,6},{6,7},{7,8},{8,9},{9,10},{10,1... | collective-permute-start | bytes 786440 | tf_op jit(solution)/shard_map/while/body/eval_jaxpr/ppermute | solution.py:16
  689.7 16.7 collective-permute-start.1
  712.7 16.7 collective-permute-start.1
  804.7 16.7 collective-permute-start.1
  827.8 16.7 collective-permute-start.1
  850.8 16.7 collective-permute-start.1
  931.4 278.8 %reduce-scatter.21.cloned.1.call-start = ((), (), s32[]{:S(2)}) async-start(), calls=%async_computation.26 | async-start | bytes 4325376
  947.9 402.7 %reduce-scatter.23.cloned.1.call-start = ((), (), s32[]{:S(2)}) async-start(), calls=%async_computation.27 | async-start | bytes 4325376
  965.3 571.0 %reduce-scatter.15.cloned.1.call-start = ((), (), s32[]{:S(2)}) async-start(), calls=%async_computation.23 | async-start | bytes 17301504 | tf_op jit(solution)/shard_map/reduce_scatter | solution.py:348
  974.9 748.3 %reduce-scatter.17.cloned.1.call-start = ((), (), s32[]{:S(2)}) async-start(), calls=%async_computation.24 | async-start | bytes 17301504 | tf_op jit(solution)/shard_map/reduce_scatter | solution.py:350
  (96 other events, 2071.3 us)
Sparse Core Ops, SparseCore 0:
  10.9 57.6 all-gather.9
  71.5 55.6 all-gather.15
  130.0 55.3 all-gather.13
  187.3 49.6 all-gather.11
  239.0 49.2 all-gather.17
  291.0 54.9 all-gather.19
  348.8 76.4 all-gather.21
  428.1 76.0 all-gather.23
  530.8 163.3 reduce-scatter.12
  931.5 138.0 reduce-scatter.18
  1072.4 137.7 reduce-scatter.20
  1212.9 137.6 reduce-scatter.22
  1353.5 182.7 reduce-scatter.14
  1539.0 184.1 reduce-scatter.16
where the time goes:
time: 1740 us; the launch traced here: 1730 us
  waiting for transfers between devices  1240 us (71%)
  blocking collectives  158 us (9%)
  local copies, waits for them, and re-layouts  118 us (7%)
  matrix products  74 us (4%)
  loops' own time  54 us (3%)
  other arithmetic  37 us (2%)
  starting transfers between devices  34.3 us (2%)
    unnamed x17, waiting for transfers between devices  319 us
    ppermute x64, waiting for transfers between devices, passed_along(): return lax.ppermute(value, axis, pairs)  247 us
    reduce_scatter x1, waiting for transfers between devices, body(): lax.psum_scatter(grad_w2, ('head', 'blk'), scatter_dimension=0, tiled=True)  187 us
    reduce_scatter x1, waiting for transfers between devices, body(): lax.psum_scatter(grad_w1, ('head', 'blk'), scatter_dimension=0, tiled=True)  186 us
    unnamed x2, blocking collectives  81.3 us
    all_gather x1, waiting for transfers between devices, body(): lax.all_gather(w_inner, ('head', 'blk'), axis=0, tiled=True)  76.9 us
    all_gather x1, waiting for transfers between devices, body(): lax.all_gather(w_outer, ('head', 'blk'), axis=0, tiled=True)  69.3 us
    all_gather x1, waiting for transfers between devices, body(): lax.all_gather(w_key, ('head', 'blk'), axis=0, tiled=True)  59.1 us
  transfers between devices with their start and end apart: 81, of which 78 were waited for; matrix products, arithmetic and copies ran while one was open for 12% of the time, Pallas kernels for 0%

commit v1 on v0

--- a/solution.py
+++ b/solution.py
@@ -3,11 +3,25 @@
 import jax.numpy as jnp
 from jax import lax
 from jax.sharding import PartitionSpec as P
+from jax.lax import all_to_all, axis_size
 
 H = 16
 HD = 64
 EPS = 1e-05
 NEG = -1e30
+
+
+def outputs_recast(local_x, dev_axis):
+    tall = jnp.concatenate(
+        all_to_all(
+            jnp.stack([local_x] * axis_size(dev_axis)),
+            axis_name=dev_axis,
+            split_axis=0,
+            concat_axis=0,
+        ),
+        axis=0,
+    )
+    return tall
 
 
 def passed_along(value, axis, steps):
@@ -122,7 +136,7 @@
         lax.all_gather(gain_attn, ("head", "blk"), axis=0, tiled=True),
         lax.all_gather(shift_attn, ("head", "blk"), axis=0, tiled=True),
         lax.all_gather(w_inner, ("head", "blk"), axis=0, tiled=True),
-        lax.all_gather(b_inner, ("head", "blk"), axis=0, tiled=True),
+        outputs_recast(b_inner, ("head", "blk")),
         lax.all_gather(w_outer, ("head", "blk"), axis=0, tiled=True),
         lax.all_gather(b_outer, ("head", "blk"), axis=0, tiled=True),
         lax.all_gather(gain_ffn, ("head", "blk"), axis=0, tiled=True),

time: 1740 us -> 1740 us (level)
  blocking collectives: 158 us -> 119 us
  waiting for transfers between devices: 1240 us -> 1270 us
    all_gather x1 -> x0, blocking collectives: 39.4 us -> none  [body(): lax.all_gather(b_inner, ('head', 'blk'), axis=0, tiled=True)]
    all_gather x1, waiting for transfers between devices: 3.66 us -> 38.3 us  [body(): key_piece = lax.all_gather(key_cols, 'blk', axis=0, tiled=True)]
  transfers between devices with their start and end apart: 81 -> 82, of which waited for: 78 -> 79; matrix products, arithmetic and copies ran while one was open for 12% -> 12% of each run, Pallas kernels for 0% -> 0%
where the time goes in v1:
time: 1740 us; the launch traced here: 1730 us
  waiting for transfers between devices  1270 us (73%)
  local copies, waits for them, and re-layouts  119 us (7%)
  blocking collectives  119 us (7%)
  matrix products  74 us (4%)
  loops' own time  54 us (3%)
  starting transfers between devices  40.9 us (2%)
  other arithmetic  37 us (2%)
    unnamed x17, waiting for transfers between devices  319 us
    ppermute x64, waiting for transfers between devices, passed_along(): return lax.ppermute(value, axis, pairs)  246 us
    reduce_scatter x1, waiting for transfers between devices, body(): lax.psum_scatter(grad_w2, ('head', 'blk'), scatter_dimension=0, tiled=True)  187 us
    reduce_scatter x1, waiting for transfers between devices, body(): lax.psum_scatter(grad_w1, ('head', 'blk'), scatter_dimension=0, tiled=True)  186 us
    unnamed x2, blocking collectives  81.5 us
    all_gather x1, waiting for transfers between devices, body(): lax.all_gather(w_inner, ('head', 'blk'), axis=0, tiled=True)  76.9 us
    all_gather x1, waiting for transfers between devices, body(): lax.all_gather(w_outer, ('head', 'blk'), axis=0, tiled=True)  69.3 us
    all_gather x1, waiting for transfers between devices, body(): lax.all_gather(w_key, ('head', 'blk'), axis=0, tiled=True)  59.1 us
  transfers between devices with their start and end apart: 82, of which 79 were waited for; matrix products, arithmetic and copies ran while one was open for 12% of the time, Pallas kernels for 0%

profile of v1, /device:TPU:4, one launch (start us, length us, event | category | flops | bytes accessed | tf_op | source)
XLA Modules:
  0.0 1729.0 jit_solution(9471488116752150321)
XLA Ops:
  9.5 59.1 %all-gather.9.cloned.1.call-done = bf16[1024,1024]{1,0:T(8,128)(2,1)} async-done(((bf16[32,1024]{1,0:T(8,128)(2,1)}), bf16[1024,1024]{1,0:T(8,128)(2,1)}) %all-gather.9.cloned.1.call-update) | async-done | bytes 2097168 | tf_op jit(solution)/shard_map/all_gather | solution.py:130
  80.6 40.7 %all-reduce.18 = (bf16[1024]{0:T(1024)(128)(2,1)S(1)}, bf16[1024]{0:T(1024)(128)(2,1)S(1)}, bf16[1024]{0:T(1024)(128)(2,1)S(1)}, bf16[1024]{0:T(1024)(128)(2,1)S...) all-reduce(bf16[1024]{0:T(1024)(128)(2,1)S(1)} %dynamic-update-slic, ...), channel_id=1, replica_groups=mesh['head'=2,'blk'=16] {'head','blk'}, use_global_device_ids=true, to_apply=%add | all-reduce | flops 8192 | bytes 32768
  144.6 40.7 %all-gather.13.cloned.1.call-done = bf16[1024,1024]{1,0:T(8,128)(2,1)} async-done(((bf16[32,1024]{1,0:T(8,128)(2,1)}), bf16[1024,1024]{1,0:T(8,128)(2,1)}) %all-gather.13.cloned.1.call-update) | async-done | bytes 2097168 | tf_op jit(solution)/shard_map/all_gather | solution.py:129
  198.5 38.3 %all-gather.11.cloned.1.call-done = bf16[4096,512]{1,0:T(8,128)(2,1)} async-done(((bf16[256,512]{1,0:T(8,128)(2,1)}), bf16[4096,512]{1,0:T(8,128)(2,1)}) %all-gather.11.cloned.1.call-update) | async-done | bytes 4194320 | tf_op jit(solution)/shard_map/all_gather | solution.py:190
  236.8 11.3 reshape.276
  248.1 9.9 copy.106
  258.0 30.1 %all-gather.17.cloned.1.call-done = bf16[4096,512]{1,0:T(8,128)(2,1)} async-done(((bf16[256,512]{1,0:T(8,128)(2,1)}), bf16[4096,512]{1,0:T(8,128)(2,1)}) %all-gather.17.cloned.1.call-update) | async-done | bytes 4194320 | tf_op jit(solution)/shard_map/all_gather | solution.py:191
  288.1 11.2 reshape.277
  299.3 9.8 copy.107
  309.1 23.4 %while.38 = (s32[]{:T(128)}, f32[8,256]{1,0:T(8,128)S(1)}, f32[8,256]{1,0:T(8,128)S(1)}, f32[8,256,64]{1,2,0:T(8,128)S(1)}, s32[4,1024]{1,0:T(4,128)S(1)}, /*ind...) while((s32[]{:T(128)}, f32[8,256]{1,0:T(8,128)S(1)}, ...), condition=%wide.region_5.6_spmd, body=%wide.region_0.5_spmd.sunk | while | flops 560467968 | bytes 29768016 | solution.py:215
  348.2 76.9 %all-gather.21.cloned.1.call-done = bf16[1024,4096]{1,0:T(8,128)(2,1)} async-done(((bf16[32,4096]{1,0:T(8,128)(2,1)}), bf16[1024,4096]{1,0:T(8,128)(2,1)}) %all-gather.21.cloned.1.call-update) | async-done | bytes 8388624 | tf_op jit(solution)/shard_map/all_gather | solution.py:138
  425.1 9.6 multiply_convert_fusion.1
  434.7 69.3 %all-gather.23.cloned.1.call-done = bf16[4096,1024]{1,0:T(8,128)(2,1)} async-done(((bf16[128,1024]{1,0:T(8,128)(2,1)}), bf16[4096,1024]{1,0:T(8,128)(2,1)}) %all-gather.23.cloned.1.call-update) | async-done | bytes 8388624 | tf_op jit(solution)/shard_map/all_gather | solution.py:140
  531.5 384.1 %while.39 = (s32[]{:T(128)}, bf16[256,8,64]{0,2,1:T(8,128)(2,1)}, bf16[256,8,64]{0,2,1:T(8,128)(2,1)S(1)}, f32[256,8,64]{0,2,1:T(8,128)S(1)}, f32[256,8,64]{0,2,...) while((s32[]{:T(128)}, bf16[256,8,64]{0,2,1:T(8,128)(2,1)}, ...), condition=%wide.region_18.19_spmd.clone, body=%wide.region_15.18_spmd.clone.sunk | while | flops 340721696 | bytes 25055948 | solution.py:312
  639.4 8.9 collective-permute-done.2
  664.4 8.5 collective-permute-done.2
  689.1 8.2 collective-permute-done.2
  712.2 8.2 collective-permute-done.2
  985.1 40.8 %all-reduce.17 = (f32[1024]{0:T(1024)S(1)}, f32[1024]{0:T(1024)S(1)}, f32[1024]{0:T(1024)S(1)}, f32[1024]{0:T(1024)S(1)}, f32[1024]{0:T(1024)S(1)}, /*index=5*/f...) all-reduce(f32[1024]{0:T(1024)S(1)} %bitcast.193, ...), channel_id=5, replica_groups=mesh['head'=2,'blk'=16] {'head','blk'}, use_global_device_ids=true, to_apply=%region_23.24.clone | all-reduce | flops 12288 | bytes 98304
  1035.3 33.7 %reduce-scatter.19.cloned.1.call-done = f32[32,1024]{1,0:T(8,128)} async-done(((f32[1024,1024]{1,0:T(8,128)}), f32[32,1024]{1,0:T(8,128)}) %reduce-scatter.19.cloned.1.call-update) | async-done | bytes 131088
  1069.0 140.6 %reduce-scatter.21.cloned.1.call-done = f32[32,1024]{1,0:T(8,128)} async-done(((f32[1024,1024]{1,0:T(8,128)}), f32[32,1024]{1,0:T(8,128)}) %reduce-scatter.21.cloned.1.call-update) | async-done | bytes 131088
  1209.5 140.1 %reduce-scatter.23.cloned.1.call-done = f32[32,1024]{1,0:T(8,128)} async-done(((f32[1024,1024]{1,0:T(8,128)}), f32[32,1024]{1,0:T(8,128)}) %reduce-scatter.23.cloned.1.call-update) | async-done | bytes 131088
  1349.7 185.6 %reduce-scatter.15.cloned.1.call-done = f32[32,4096]{1,0:T(8,128)} async-done(((f32[1024,4096]{1,0:T(8,128)}), f32[32,4096]{1,0:T(8,128)}) %reduce-scatter.15.cloned.1.call-update) | async-done | bytes 524304 | tf_op jit(solution)/shard_map/reduce_scatter | solution.py:362
  1535.3 187.0 %reduce-scatter.17.cloned.1.call-done = f32[128,1024]{1,0:T(8,128)} async-done(((f32[4096,1024]{1,0:T(8,128)}), f32[128,1024]{1,0:T(8,128)}) %reduce-scatter.17.cloned.1.call-update) | async-done | bytes 524304 | tf_op jit(solution)/shard_map/reduce_scatter | solution.py:364
  (567 shorter events, 505.3 us)
Async XLA Ops:
  7.3 61.4 %all-gather.9.cloned.1.call-start = ((), (), s32[]{:S(2)}) async-start(), calls=%async_computation.15 | async-start | bytes 2162688 | tf_op jit(solution)/shard_map/all_gather | solution.py:130
  8.0 119.1 %all-gather.15.cloned.1.call-start = ((), (), s32[]{:S(2)}) async-start(), calls=%async_computation.18 | async-start | bytes 2162688 | tf_op jit(solution)/shard_map/all_gather | solution.py:131
  8.8 176.6 %all-gather.13.cloned.1.call-start = ((), (), s32[]{:S(2)}) async-start(), calls=%async_computation.17 | async-start | bytes 2162688 | tf_op jit(solution)/shard_map/all_gather | solution.py:129
  9.5 227.3 %all-gather.11.cloned.1.call-start = ((), (), s32[]{:S(2)}) async-start(), calls=%async_computation.16 | async-start | bytes 4456448 | tf_op jit(solution)/shard_map/all_gather | solution.py:190
  78.6 209.5 %all-gather.17.cloned.1.call-start = ((), (), s32[]{:S(2)}) async-start(), calls=%async_computation.19 | async-start | bytes 4456448 | tf_op jit(solution)/shard_map/all_gather | solution.py:191
  137.0 208.8 %all-gather.19.cloned.1.call-start = ((), (), s32[]{:S(2)}) async-start(), calls=%async_computation.20 | async-start | bytes 2162688 | tf_op jit(solution)/shard_map/all_gather | solution.py:134
  137.6 287.5 %all-gather.21.cloned.1.call-start = ((), (), s32[]{:S(2)}) async-start(), calls=%async_computation.21 | async-start | bytes 8650752 | tf_op jit(solution)/shard_map/all_gather | solution.py:138
  138.4 365.7 %all-gather.23.cloned.1.call-start = ((), (), s32[]{:S(2)}) async-start(), calls=%async_computation.22 | async-start | bytes 8650752 | tf_op jit(solution)/shard_map/all_gather | solution.py:140
  139.7 48.4 %all-to-all-start.4 = ((bf16[32,1,128]{2,1,0:T(2,128)(2,1)}), bf16[32,1,128]{2,1,0:T(2,128)(2,1)S(1)}, u32[]{:S(2)}, u32[]{:S(2)}) async-start(bf16[32,1,128]{2,1,0:T(2,128)(2,1)} %stack.2), calls=%async_computation.4 | async-start | bytes 32768 | tf_op jit(solution)/shard_map/all_to_all | solution.py:16
  526.9 508.4 %reduce-scatter.13.cloned.1.call-start = ((), (), s32[]{:S(2)}) async-start(), calls=%async_computation.23 | async-start | bytes 4325376 | tf_op jit(solution)/shard_map/reduce_scatter | solution.py:358
  529.9 539.1 %reduce-scatter.19.cloned.1.call-start = ((), (), s32[]{:S(2)}) async-start(), calls=%async_computation.26 | async-start | bytes 4325376
  589.8 18.0 %collective-permute-start.1 = (bf16[256,8,64]{0,2,1:T(8,128)(2,1)S(1)}, bf16[256,8,64]{0,2,1:T(8,128)(2,1)S(1)}, u32[]{:S(2)}, u32[]{:S(2)}) collective-permute-start(bf16[256,8,64]{0,2,1:T(8,128)(2,1)S(1)} %copy.190), channel_id=1, source_target_pairs={{0,1},{1,2},{2,3},{3,4},{4,5},{5,6},{6,7},{7,8},{8,9},{9,10},{10,1... | collective-permute-start | bytes 786440 | tf_op jit(solution)/shard_map/while/body/eval_jaxpr/ppermute | solution.py:30
  614.1 18.9 %collective-permute-start.1 = (bf16[256,8,64]{0,2,1:T(8,128)(2,1)S(1)}, bf16[256,8,64]{0,2,1:T(8,128)(2,1)S(1)}, u32[]{:S(2)}, u32[]{:S(2)}) collective-permute-start(bf16[256,8,64]{0,2,1:T(8,128)(2,1)S(1)} %copy.190), channel_id=1, source_target_pairs={{0,1},{1,2},{2,3},{3,4},{4,5},{5,6},{6,7},{7,8},{8,9},{9,10},{10,1... | collective-permute-start | bytes 786440 | tf_op jit(solution)/shard_map/while/body/eval_jaxpr/ppermute | solution.py:30
  639.3 18.8 %collective-permute-start.1 = (bf16[256,8,64]{0,2,1:T(8,128)(2,1)S(1)}, bf16[256,8,64]{0,2,1:T(8,128)(2,1)S(1)}, u32[]{:S(2)}, u32[]{:S(2)}) collective-permute-start(bf16[256,8,64]{0,2,1:T(8,128)(2,1)S(1)} %copy.190), channel_id=1, source_target_pairs={{0,1},{1,2},{2,3},{3,4},{4,5},{5,6},{6,7},{7,8},{8,9},{9,10},{10,1... | collective-permute-start | bytes 786440 | tf_op jit(solution)/shard_map/while/body/eval_jaxpr/ppermute | solution.py:30
  664.4 18.4 %collective-permute-start.1 = (bf16[256,8,64]{0,2,1:T(8,128)(2,1)S(1)}, bf16[256,8,64]{0,2,1:T(8,128)(2,1)S(1)}, u32[]{:S(2)}, u32[]{:S(2)}) collective-permute-start(bf16[256,8,64]{0,2,1:T(8,128)(2,1)S(1)} %copy.190), channel_id=1, source_target_pairs={{0,1},{1,2},{2,3},{3,4},{4,5},{5,6},{6,7},{7,8},{8,9},{9,10},{10,1... | collective-permute-start | bytes 786440 | tf_op jit(solution)/shard_map/while/body/eval_jaxpr/ppermute | solution.py:30
  689.1 16.7 collective-permute-start.1
  735.1 16.7 collective-permute-start.1
  758.1 16.7 collective-permute-start.1
  781.1 16.7 collective-permute-start.1
  898.9 16.7 collective-permute-start.1
  930.9 278.6 %reduce-scatter.21.cloned.1.call-start = ((), (), s32[]{:S(2)}) async-start(), calls=%async_computation.27 | async-start | bytes 4325376
  947.5 402.2 %reduce-scatter.23.cloned.1.call-start = ((), (), s32[]{:S(2)}) async-start(), calls=%async_computation.28 | async-start | bytes 4325376
  964.8 570.4 %reduce-scatter.15.cloned.1.call-start = ((), (), s32[]{:S(2)}) async-start(), calls=%async_computation.24 | async-start | bytes 17301504 | tf_op jit(solution)/shard_map/reduce_scatter | solution.py:362
  974.4 747.8 %reduce-scatter.17.cloned.1.call-start = ((), (), s32[]{:S(2)}) async-start(), calls=%async_computation.25 | async-start | bytes 17301504 | tf_op jit(solution)/shard_map/reduce_scatter | solution.py:364
  (97 other events, 1928.2 us)
Sparse Core Ops, SparseCore 0:
  10.9 57.6 all-gather.8
  71.5 55.6 all-gather.14
  130.0 55.3 all-gather.12
  187.4 49.4 all-gather.10
  238.8 49.2 all-gather.16
  290.8 54.9 all-gather.18
  348.6 76.4 all-gather.20
  427.9 76.0 all-gather.22
  530.6 162.5 reduce-scatter.12
  931.0 137.9 reduce-scatter.18
  1071.8 137.6 reduce-scatter.20
  1212.2 137.3 reduce-scatter.22
  1352.5 182.6 reduce-scatter.14
  1538.0 184.1 reduce-scatter.16
